TPU v7x, 32 devices: a whole 2x2x4 slice. The times are simulated.
32 devices in a mesh: tok: 2 (over core), head: 4 (over y, x), exp: 4 (over z).
Axes of the slice: x: 2, y: 2, z: 4, core: 2. Of those that a mesh axis runs over, the one named last changes fastest.
Arguments:
- context: bfloat16 [4, 64, 4096], P('exp', 'tok', 'head'), may hold values from -6 to 6
- out_proj: bfloat16 [4096, 4096], P('head', 'exp'), may hold values from -0.125 to 0.125
- stream: float32 [4, 64, 4096], P('exp', 'tok', 'head'), may hold values from -75 to 75
- norm_gain: float32 [4096], replicated, may hold values from 0.1 to 1.9
- expert_ids: int32 [4, 64, 8], P('exp', 'tok'), may hold values from 0 to 31, as said below
- slot_ids: int32 [4, 64, 8], P('exp', 'tok'), may hold values from -1 to 11, as said below
- gate_probs: float32 [4, 64, 8], P('exp', 'tok'), may hold values from 0.02 to 0.3
- w_gate: bfloat16 [32, 3072, 4096], P(('tok', 'exp'), 'head'), may hold values from -0.09375 to 0.09375
- w_up: bfloat16 [32, 3072, 4096], P(('tok', 'exp'), 'head'), may hold values from -0.09375 to 0.09375
- w_down: bfloat16 [32, 3072, 4096], P(('tok', 'exp'), 'head'), may hold values from -0.15625 to 0.15625
Outputs:
- mixed: float32 [4, 64, 4096], P('exp', 'tok', 'head')
Inputs may be any that keep to these rules, and one draw needn't show every extreme that they name: `expert_ids`: each token names 8 different experts. `slot_ids`: within a block of 32 consecutive tokens of one image, the choices of one expert take slots 0, 1, 2, ... in token order until its 12 slots are full, later ones get -1; in every block some expert fills all 12 slots.
All inputs are finite; a program needn't handle non-finite values.
Results may differ from a plain program's by a relative error of at most 0.0034.
Values may be sent and summed in bfloat16 or wider, within the bound.
A program may use at most 128 MiB of HBM per device.

v0:
```python
import jax
import jax.numpy as jnp
from jax import lax
from jax.sharding import PartitionSpec as P

EXPERTS = 32
TOP = 8
CAP = 12
eps_value = 1e-05


def on_device(
    context, out_proj, stream, norm_gain, expert_ids, slot_ids, gate_probs, w_gate, w_up, w_down
):
    local_context = context[0]
    own_stream = stream[0]
    col_width = own_stream.shape[1]
    col_start = lax.axis_index("head") * col_width
    partial_value = jnp.dot(
        local_context,
        lax.all_gather(out_proj, "exp", axis=1, tiled=True),
        preferred_element_type=jnp.float32,
    )
    own_sum = lax.dynamic_slice_in_dim(partial_value, col_start, col_width, 1) + own_stream
    partial_value = lax.dynamic_update_slice_in_dim(partial_value, own_sum, col_start, 1)
    resid_full = lax.psum(partial_value, "head")
    resid_own = lax.dynamic_slice_in_dim(resid_full, col_start, col_width, 1)
    mean_sq = jnp.mean(resid_full * resid_full, axis=1, keepdims=True)
    gain_own = lax.dynamic_slice_in_dim(norm_gain, col_start, col_width, 0)
    normed_own = (resid_own * lax.rsqrt(mean_sq + eps_value) * gain_own).astype(jnp.bfloat16)
    choice_ids = expert_ids[0]
    choice_slots = slot_ids[0]
    weights = gate_probs[0]
    spill_slot = EXPERTS * CAP
    target = jnp.where(choice_slots >= 0, choice_ids * CAP + choice_slots, spill_slot)
    outgoing = (
        jnp.zeros((spill_slot + 1, col_width), jnp.bfloat16)
        .at[target.reshape(-1)]
        .set(jnp.repeat(normed_own, TOP, axis=0))
    )
    outgoing = outgoing[:spill_slot].reshape(EXPERTS, CAP, col_width)
    tok_count = lax.axis_size("tok")
    groups = tok_count * lax.axis_size("exp")
    local_experts = w_gate.shape[0]
    arrived = lax.all_to_all(outgoing, ("tok", "exp"), split_axis=0, concat_axis=0, tiled=True)
    arrived = arrived.reshape(groups, local_experts, CAP, col_width)
    piece = lax.all_gather(arrived, "head", axis=3, tiled=True)
    gate_more = jnp.einsum("slcd,lhd->slch", piece, w_gate, preferred_element_type=jnp.float32)
    up_more = jnp.einsum("slcd,lhd->slch", piece, w_up, preferred_element_type=jnp.float32)
    hidden = (jax.nn.silu(gate_more) * up_more).astype(jnp.bfloat16)
    produced = jnp.einsum(
        "slch,lhd->slcd", hidden, w_down, preferred_element_type=jnp.float32
    ).astype(jnp.bfloat16)
    widened = lax.optimization_barrier(produced).astype(jnp.float32)
    summed = lax.psum_scatter(
        widened.astype(jnp.bfloat16), "head", scatter_dimension=3, tiled=True
    ).astype(jnp.float32)
    returned_share = lax.all_to_all(
        summed.reshape(EXPERTS, CAP, col_width).astype(jnp.bfloat16),
        ("tok", "exp"),
        split_axis=0,
        concat_axis=0,
        tiled=True,
    ).astype(jnp.float32)
    lookup_share = jnp.concatenate(
        [returned_share.reshape(spill_slot, col_width), jnp.zeros((1, col_width), jnp.float32)],
        axis=0,
    )
    picked_share = lookup_share[target]
    expert_own = jnp.sum(picked_share * weights[:, :, None], axis=1)
    return (resid_own + expert_own)[None]


def solution(mesh):
    in_specs = (
        P("exp", "tok", "head"),
        P("head", "exp"),
        P("exp", "tok", "head"),
        P(),
        P("exp", "tok", None),
        P("exp", "tok", None),
        P("exp", "tok", None),
        P(("tok", "exp"), "head", None),
        P(("tok", "exp"), "head", None),
        P(("tok", "exp"), "head", None),
    )
    out_specs = P("exp", "tok", "head")
    return jax.shard_map(
        on_device, mesh=mesh, in_specs=in_specs, out_specs=out_specs, check_vma=False
    )
```

profile of v0, /device:TPU:0, one launch (start us, length us, event | category | flops | bytes accessed | tf_op | source)
XLA Modules:
  0.0 433.1 jit_solution(15233698592753137792)
XLA Ops:
  6.5 0.7 all-gather.3.cloned.1.call-update
  7.4 153.9 %all-gather.3.cloned.1.call-done = bf16[1024,4096]{1,0:T(8,128)(2,1)} async-done(((bf16[1024,1024]{1,0:T(8,128)(2,1)}), bf16[1024,4096]{1,0:T(8,128)(2,1)}) %all-gather.3.cloned.1.call-update) | async-done | bytes 8388624 | tf_op jit(solution)/shard_map/all_gather | solution.py:21
  161.3 4.9 %fusion.24 = f32[32,4096]{1,0:T(8,128)S(1)} fusion(bf16[1024,4096]{1,0:T(8,128)(2,1)} %all-gather.3.cloned.1.call-done, bf16[1,32,1024]{2,1,0:T(8,128)(2,1)S(1)} %copy-done), kind=kOutput, calls=%fused_computation.29 | convolution fusion | flops 268435456 | bytes 8978432 | tf_op jit(solution)/shard_map/dot_general | solution.py:19
  166.2 0.8 copy-done.2
  167.1 0.0 all-gather.5.cloned.1.call-start
  167.1 0.1 copy.19
  167.2 0.1 select_n.53
  167.3 43.5 %all-reduce.3.cloned.1.call-done = f32[32,4096]{1,0:T(8,128)} async-done(((f32[32,4096]{1,0:T(8,128)}), f32[32,4096]{1,0:T(8,128)}) %all-reduce.3.cloned.1.call-update) | async-done | bytes 524304 | tf_op jit(solution)/shard_map/psum | solution.py:26
  210.8 1.2 multiply_reduce_fusion
  212.0 1.0 multiply_convert_fusion
  213.0 1.9 scatter_custom_fusion
  214.9 0.1 slice.6
  214.9 0.2 reshape.125
  215.1 30.6 %all_to_all.10 = bf16[32,12,1024]{2,1,0:T(8,128)(2,1)S(1)} all-to-all(bf16[32,12,1024]{2,1,0:T(8,128)(2,1)S(1)} %reshape.125), channel_id=1, replica_groups=mesh['tok'=2,'head'=4,'exp'=4] {'tok','exp'}, dimensions={0} | all-to-all | bytes 1572864 | tf_op jit(solution)/shard_map/all_to_all | solution.py:45
  245.7 1.0 copy.21
  246.8 0.2 reduce-scatter.2.cloned.1.call-start
  247.0 50.0 %all-gather.5.cloned.1.call-done = bf16[8,4,12,4096]{3,2,0,1:T(8,128)(2,1)} async-done(((bf16[8,4,12,1024]{3,2,0,1:T(8,128)(2,1)}), bf16[8,4,12,4096]{3,2,0,1:T(8,128)(2,1)}) %all-gather.5.cloned.1.call-update) | async-done | bytes 3145744 | tf_op jit(solution)/shard_map/all_gather | solution.py:47
  297.0 13.4 %fusion.4 = f32[4,8,12,768]{3,2,1,0:T(8,128)S(1)} fusion(bf16[8,4,12,4096]{3,2,0,1:T(8,128)(2,1)} %all-gather.5.cloned.1.call-done, bf16[4,768,4096]{2,1,0:T(8,128)(2,1)} %param.17), kind=kOutput, calls=%fused_computation.6 | convolution fusion | flops 2415919104 | bytes 29491200 | tf_op jit(solution)/shard_map/slcd,lhd->slch/dot_general | solution.py:48
  310.4 13.5 %fusion.12 = bf16[8,4,12,768]{3,2,0,1:T(8,128)(2,1)S(1)} fusion(f32[4,8,12,768]{3,2,1,0:T(8,128)S(1)} %fusion.4, bf16[8,4,12,4096]{3,2,0,1:T(8,128)(2,1)} %all-gather.5.cloned.1.call-done, bf16[4,768,4096]{2,1,0:T(8,128)(2,1)} %param.18), kind=kOutput, calls=%fused_computation.11 | convolution fusion | flops 2417688576 | bytes 30081024 | tf_op jit(solution)/shard_map/slcd,lhd->slch/dot_general | solution.py:49
  323.9 13.6 %fusion.9 = bf16[8,4,12,4096]{3,2,0,1:T(8,128)(2,1)} fusion(bf16[8,4,12,768]{3,2,0,1:T(8,128)(2,1)S(1)} %fusion.12, bf16[4,768,4096]{2,1,0:T(8,128)(2,1)} %param.19), kind=kOutput, calls=%fused_computation.9 | convolution fusion | flops 2417491968 | bytes 28901376 | tf_op jit(solution)/shard_map/slch,lhd->slcd/dot_general | solution.py:51
  337.5 52.7 %reduce-scatter.2.cloned.1.call-done = bf16[8,4,12,1024]{3,2,0,1:T(8,128)(2,1)} async-done(((bf16[8,4,12,4096]{3,2,0,1:T(8,128)(2,1)}), bf16[8,4,12,1024]{3,2,0,1:T(8,128)(2,1)}) %reduce-scatter.2.cloned.1.call-update) | async-done | bytes 786448 | tf_op jit(solution)/shard_map/reduce_scatter | solution.py:55
  390.2 2.3 copy.31
  392.5 4.6 %all-to-all-start.1 = ((bf16[32,12,1024]{2,1,0:T(8,128)(2,1)}), bf16[32,12,1024]{2,1,0:T(8,128)(2,1)S(1)}, u32[]{:S(2)}, u32[]{:S(2)}) async-start(bf16[32,12,1024]{2,1,0:T(8,128)(2,1)} %bitcast.14), calls=%async_computation.2 | async-start | bytes 2097152 | tf_op jit(solution)/shard_map/all_to_all | solution.py:58
  397.1 0.1 copy.24
  397.2 0.1 reshape.130
  397.3 0.1 copy.25
  397.4 25.7 %all-to-all-done.1 = bf16[32,12,1024]{2,1,0:T(8,128)(2,1)S(1)} async-done(((bf16[32,12,1024]{2,1,0:T(8,128)(2,1)}), bf16[32,12,1024]{2,1,0:T(8,128)(2,1)S(1)}, u32[]{:S(2)}, u32[]{:S(2)}) %all-to-all-start.1) | async-done | bytes 786464 | tf_op jit(solution)/shard_map/all_to_all | solution.py:58
  423.1 0.2 reshape.127
  423.3 0.2 pad_convert_fusion
  423.5 1.1 gather_fusion
  424.6 0.4 fusion.18
  424.9 1.6 add_bitcast_fusion
  (25 shorter events, 0.2 us)
Async XLA Ops:
  6.5 154.7 %copy-start = (bf16[1,32,1024]{2,1,0:T(8,128)(2,1)S(1)}, bf16[1,32,1024]{2,1,0:T(8,128)(2,1)}, u32[]{:S(2)}) copy-start(bf16[1,32,1024]{2,1,0:T(8,128)(2,1)} %param.10) | copy-start | bytes 196612
  6.5 154.7 %all-gather.3.cloned.1.call-start = ((), (), s32[]{:S(2)}) async-start(), calls=%async_computation.3 | async-start | bytes 10485760 | tf_op jit(solution)/shard_map/all_gather | solution.py:21
  7.3 203.5 %all-reduce.3.cloned.1.call-start = ((), (), s32[]{:S(2)}) async-start(), calls=%async_computation.4 | async-start | bytes 1048576 | tf_op jit(solution)/shard_map/psum | solution.py:26
  7.3 158.9 %copy-start.3 = (f32[1,32,1024]{2,1,0:T(8,128)S(1)}, f32[1,32,1024]{2,1,0:T(8,128)}, u32[]{:S(2)}) copy-start(f32[1,32,1024]{2,1,0:T(8,128)} %param.12) | copy-start | bytes 393220
  7.3 159.8 %copy-start.5 = (s32[1,32,8]{1,2,0:T(8,128)S(1)}, s32[1,32,8]{1,2,0:T(8,128)}, u32[]{:S(2)}) copy-start(s32[1,32,8]{1,2,0:T(8,128)} %param.15) | copy-start | bytes 3076
  7.3 159.8 %copy-start.6 = (s32[1,32,8]{1,2,0:T(8,128)S(1)}, s32[1,32,8]{1,2,0:T(8,128)}, u32[]{:S(2)}) copy-start(s32[1,32,8]{1,2,0:T(8,128)} %param.14) | copy-start | bytes 3076
  7.3 204.6 %dynamic-slice-start = ((f32[4096]{0:T(1024)}, s32[]{:T(128)}), f32[1024]{0:T(1024)S(1)}, s32[]{:S(2)}) async-start(f32[4096]{0:T(1024)} %param.13, s32[]{:T(128)} %select_n.51), calls=%async_computation.7 | async-start | bytes 8704 | tf_op jit(solution)/shard_map/dynamic_slice | solution.py:29
  166.2 0.8 copy-start.2
  167.1 129.9 %all-gather.5.cloned.1.call-start = ((), (), s32[]{:S(2)}) async-start(), calls=%async_computation.5 | async-start | bytes 5242880 | tf_op jit(solution)/shard_map/all_gather | solution.py:47
  246.8 143.4 %reduce-scatter.2.cloned.1.call-start = ((), (), s32[]{:S(2)}) async-start(), calls=%async_computation.6 | async-start | bytes 5242880 | tf_op jit(solution)/shard_map/reduce_scatter | solution.py:55
  337.5 59.8 %copy-start.4 = (f32[1,32,8]{1,2,0:T(8,128)S(1)}, f32[1,32,8]{1,2,0:T(8,128)}, u32[]{:S(2)}) copy-start(f32[1,32,8]{1,2,0:T(8,128)} %param.16) | copy-start | bytes 3076
  392.5 30.6 %all-to-all-start.1 = ((bf16[32,12,1024]{2,1,0:T(8,128)(2,1)}), bf16[32,12,1024]{2,1,0:T(8,128)(2,1)S(1)}, u32[]{:S(2)}, u32[]{:S(2)}) async-start(bf16[32,12,1024]{2,1,0:T(8,128)(2,1)} %bitcast.14), calls=%async_computation.2 | async-start | bytes 2097152 | tf_op jit(solution)/shard_map/all_to_all | solution.py:58
  423.3 3.2 copy-start.1
Sparse Core Ops, SparseCore 0:
  8.9 152.3 all-gather.2
  167.2 43.5 all-reduce.2
  246.9 50.0 all-gather.4
  337.6 52.5 reduce-scatter.1
where the time goes:
time: 433 us
  waiting for transfers between devices  327 us (76%)
  matrix products  45.4 us (10%)
  blocking collectives  30.6 us (7%)
  between operations  13.3 us (3%)
  local copies, waits for them, and re-layouts  7.94 us (2%)
  starting transfers between devices  4.91 us (1%)
  other arithmetic  4.33 us (1%)
    all_gather x1, waiting for transfers between devices, on_device(): lax.all_gather(out_proj, 'exp', axis=1, tiled=True)  154 us
    reduce_scatter x1, waiting for transfers between devices, on_device(): lax.psum_scatter(widened.astype(jnp.bfloat16), 'head', scatter_dimension=...  52.7 us
    all_gather x1, waiting for transfers between devices, on_device(): piece = lax.all_gather(arrived, 'head', axis=3, tiled=True)  50 us
    psum x1, waiting for transfers between devices, on_device(): resid_full = lax.psum(partial_value, 'head')  43.5 us
    all_to_all x1, blocking collectives, on_device(): lax.all_to_all(outgoing, ('tok', 'exp'), split_axis=0, concat_axis=0, til...  30.6 us
    all_to_all x1, waiting for transfers between devices, on_device(): lax.all_to_all(summed.reshape(EXPERTS, CAP, col_width).astype(jnp.bfloat1...  25.7 us
    dot_general x1, matrix products, on_device(): jnp.einsum('slch,lhd->slcd', hidden, w_down, preferred_element_type=jnp.f...  13.6 us
    dot_general x1, matrix products, on_device(): jnp.einsum('slcd,lhd->slch', piece, w_up, preferred_element_type=jnp.floa...  13.5 us
  transfers between devices with their start and end apart: 5, of which 5 were waited for; matrix products, arithmetic and copies ran while one was open for 0% of the time, Pallas kernels for 0%

commit v1 on v0

--- a/solution.py
+++ b/solution.py
@@ -23,7 +23,11 @@
     )
     own_sum = lax.dynamic_slice_in_dim(partial_value, col_start, col_width, 1) + own_stream
     partial_value = lax.dynamic_update_slice_in_dim(partial_value, own_sum, col_start, 1)
-    resid_full = lax.psum(partial_value, "head")
+    resid_full = partial_value
+    for hop in (1, 2):
+        resid_full = resid_full + lax.ppermute(
+            resid_full, "head", [(dev, dev ^ hop) for dev in range(4)]
+        )
     resid_own = lax.dynamic_slice_in_dim(resid_full, col_start, col_width, 1)
     mean_sq = jnp.mean(resid_full * resid_full, axis=1, keepdims=True)
     gain_own = lax.dynamic_slice_in_dim(norm_gain, col_start, col_width, 0)

time: 433 us -> 412 us (0.952)
  waiting for transfers between devices: 327 us -> 308 us
    psum x1 -> x0, waiting for transfers between devices: 43.5 us -> none  [on_device(): resid_full = lax.psum(partial_value, 'head')]
    ppermute x0 -> x2, waiting for transfers between devices: none -> 23.7 us  [on_device(): lax.ppermute(resid_full, 'head', [(dev, dev ^ hop) for dev in range(4)])]
  transfers between devices with their start and end apart: 5 -> 6, of which waited for: 5 -> 6; matrix products, arithmetic and copies ran while one was open for 0% -> 0% of each run, Pallas kernels for 0% -> 0%
where the time goes in v1:
time: 412 us
  waiting for transfers between devices  308 us (75%)
  matrix products  45.4 us (11%)
  blocking collectives  28.6 us (7%)
  between operations  13.3 us (3%)
  starting transfers between devices  7.94 us (2%)
  local copies, waits for them, and re-layouts  7.16 us (2%)
    all_gather x1, waiting for transfers between devices, on_device(): lax.all_gather(out_proj, 'exp', axis=1, tiled=True)  154 us
    reduce_scatter x1, waiting for transfers between devices, on_device(): lax.psum_scatter(widened.astype(jnp.bfloat16), 'head', scatter_dimension=...  52.8 us
    all_gather x1, waiting for transfers between devices, on_device(): piece = lax.all_gather(arrived, 'head', axis=3, tiled=True)  50.9 us
    all_to_all x1, blocking collectives, on_device(): lax.all_to_all(outgoing, ('tok', 'exp'), split_axis=0, concat_axis=0, til...  28.6 us
    all_to_all x1, waiting for transfers between devices, on_device(): lax.all_to_all(summed.reshape(EXPERTS, CAP, col_width).astype(jnp.bfloat1...  25.7 us
    ppermute x2, waiting for transfers between devices, on_device(): lax.ppermute(resid_full, 'head', [(dev, dev ^ hop) for dev in range(4)])  23.7 us
    dot_general x1, matrix products, on_device(): jnp.einsum('slch,lhd->slcd', hidden, w_down, preferred_element_type=jnp.f...  13.6 us
    dot_general x1, matrix products, on_device(): jnp.einsum('slcd,lhd->slch', piece, w_up, preferred_element_type=jnp.floa...  13.5 us
  transfers between devices with their start and end apart: 6, of which 6 were waited for; matrix products, arithmetic and copies ran while one was open for 0% of the time, Pallas kernels for 0%

profile of v1, /device:TPU:0, one launch (start us, length us, event | category | flops | bytes accessed | tf_op | source)
XLA Modules:
  0.0 411.7 jit_solution(11642829825297371412)
XLA Ops:
  6.5 0.7 all-gather.3.cloned.1.call-update
  7.4 153.9 %all-gather.3.cloned.1.call-done = bf16[1024,4096]{1,0:T(8,128)(2,1)} async-done(((bf16[1024,1024]{1,0:T(8,128)(2,1)}), bf16[1024,4096]{1,0:T(8,128)(2,1)}) %all-gather.3.cloned.1.call-update) | async-done | bytes 8388624 | tf_op jit(solution)/shard_map/all_gather | solution.py:21
  161.3 4.9 %fusion.24 = f32[32,4096]{1,0:T(8,128)S(1)} fusion(bf16[1024,4096]{1,0:T(8,128)(2,1)} %all-gather.3.cloned.1.call-done, bf16[1,32,1024]{2,1,0:T(8,128)(2,1)S(1)} %copy-done), kind=kOutput, calls=%fused_computation.29 | convolution fusion | flops 268435456 | bytes 8978432 | tf_op jit(solution)/shard_map/dot_general | solution.py:19
  166.2 1.5 collective-permute-start
  167.8 12.4 %collective-permute-done = f32[32,4096]{1,0:T(8,128)S(1)} collective-permute-done((f32[32,4096]{1,0:T(8,128)S(1)}, f32[32,4096]{1,0:T(8,128)S(1)}, u32[]{:S(2)}, u32[]{:S(2)}) %collective-permute-start) | collective-permute-done | bytes 524320 | tf_op jit(solution)/shard_map/ppermute | solution.py:28
  180.1 0.1 add.85
  180.2 1.5 collective-permute-start.1
  181.8 0.1 copy.19
  181.8 0.1 select_n.53
  181.9 11.3 %collective-permute-done.1 = f32[32,4096]{1,0:T(8,128)S(1)} collective-permute-done((f32[32,4096]{1,0:T(8,128)S(1)}, f32[32,4096]{1,0:T(8,128)S(1)}, u32[]{:S(2)}, u32[]{:S(2)}) %collective-permute-start.1) | collective-permute-done | bytes 524320 | tf_op jit(solution)/shard_map/ppermute | solution.py:28
  193.3 0.2 multiply_reduce_fusion
  193.5 0.1 multiply_convert_fusion
  193.5 1.9 scatter_custom_fusion
  195.5 0.2 reshape.125
  195.7 28.6 %all_to_all.10 = bf16[32,12,1024]{2,1,0:T(8,128)(2,1)S(1)} all-to-all(bf16[32,12,1024]{2,1,0:T(8,128)(2,1)S(1)} %reshape.125), channel_id=1, replica_groups=mesh['tok'=2,'head'=4,'exp'=4] {'tok','exp'}, dimensions={0} | all-to-all | bytes 1572864 | tf_op jit(solution)/shard_map/all_to_all | solution.py:49
  224.3 1.0 copy.21
  225.4 0.2 reduce-scatter.2.cloned.1.call-start
  225.6 50.9 %all-gather.5.cloned.1.call-done = bf16[8,4,12,4096]{3,2,0,1:T(8,128)(2,1)} async-done(((bf16[8,4,12,1024]{3,2,0,1:T(8,128)(2,1)}), bf16[8,4,12,4096]{3,2,0,1:T(8,128)(2,1)}) %all-gather.5.cloned.1.call-update) | async-done | bytes 3145744 | tf_op jit(solution)/shard_map/all_gather | solution.py:51
  276.5 13.4 %fusion.4 = f32[4,8,12,768]{3,2,1,0:T(8,128)S(1)} fusion(bf16[8,4,12,4096]{3,2,0,1:T(8,128)(2,1)} %all-gather.5.cloned.1.call-done, bf16[4,768,4096]{2,1,0:T(8,128)(2,1)} %param.17), kind=kOutput, calls=%fused_computation.6 | convolution fusion | flops 2415919104 | bytes 29491200 | tf_op jit(solution)/shard_map/slcd,lhd->slch/dot_general | solution.py:52
  289.9 13.5 %fusion.12 = bf16[8,4,12,768]{3,2,0,1:T(8,128)(2,1)S(1)} fusion(f32[4,8,12,768]{3,2,1,0:T(8,128)S(1)} %fusion.4, bf16[8,4,12,4096]{3,2,0,1:T(8,128)(2,1)} %all-gather.5.cloned.1.call-done, bf16[4,768,4096]{2,1,0:T(8,128)(2,1)} %param.18), kind=kOutput, calls=%fused_computation.11 | convolution fusion | flops 2417688576 | bytes 30081024 | tf_op jit(solution)/shard_map/slcd,lhd->slch/dot_general | solution.py:53
  303.4 13.6 %fusion.9 = bf16[8,4,12,4096]{3,2,0,1:T(8,128)(2,1)} fusion(bf16[8,4,12,768]{3,2,0,1:T(8,128)(2,1)S(1)} %fusion.12, bf16[4,768,4096]{2,1,0:T(8,128)(2,1)} %param.19), kind=kOutput, calls=%fused_computation.9 | convolution fusion | flops 2417491968 | bytes 28901376 | tf_op jit(solution)/shard_map/slch,lhd->slcd/dot_general | solution.py:55
  317.0 52.8 %reduce-scatter.2.cloned.1.call-done = bf16[8,4,12,1024]{3,2,0,1:T(8,128)(2,1)} async-done(((bf16[8,4,12,4096]{3,2,0,1:T(8,128)(2,1)}), bf16[8,4,12,1024]{3,2,0,1:T(8,128)(2,1)}) %reduce-scatter.2.cloned.1.call-update) | async-done | bytes 786448 | tf_op jit(solution)/shard_map/reduce_scatter | solution.py:59
  369.8 2.3 copy.31
  372.1 4.6 %all-to-all-start.1 = ((bf16[32,12,1024]{2,1,0:T(8,128)(2,1)}), bf16[32,12,1024]{2,1,0:T(8,128)(2,1)S(1)}, u32[]{:S(2)}, u32[]{:S(2)}) async-start(bf16[32,12,1024]{2,1,0:T(8,128)(2,1)} %bitcast.14), calls=%async_computation.2 | async-start | bytes 2097152 | tf_op jit(solution)/shard_map/all_to_all | solution.py:62
  376.8 0.1 reshape.130
  376.8 0.1 copy.25
  376.9 25.7 %all-to-all-done.1 = bf16[32,12,1024]{2,1,0:T(8,128)(2,1)S(1)} async-done(((bf16[32,12,1024]{2,1,0:T(8,128)(2,1)}), bf16[32,12,1024]{2,1,0:T(8,128)(2,1)S(1)}, u32[]{:S(2)}, u32[]{:S(2)}) %all-to-all-start.1) | async-done | bytes 786464 | tf_op jit(solution)/shard_map/all_to_all | solution.py:62
  402.7 0.2 reshape.127
  402.9 0.2 pad_convert_fusion
  403.0 1.1 gather_fusion
  404.1 0.4 fusion.18
  404.5 0.7 add_bitcast_fusion
  (25 shorter events, 0.3 us)
Async XLA Ops:
  6.5 154.7 %copy-start = (bf16[1,32,1024]{2,1,0:T(8,128)(2,1)S(1)}, bf16[1,32,1024]{2,1,0:T(8,128)(2,1)}, u32[]{:S(2)}) copy-start(bf16[1,32,1024]{2,1,0:T(8,128)(2,1)} %param.10) | copy-start | bytes 196612
  6.5 154.7 %all-gather.3.cloned.1.call-start = ((), (), s32[]{:S(2)}) async-start(), calls=%async_computation.3 | async-start | bytes 10485760 | tf_op jit(solution)/shard_map/all_gather | solution.py:21
  7.3 269.2 %all-gather.5.cloned.1.call-start = ((), (), s32[]{:S(2)}) async-start(), calls=%async_computation.4 | async-start | bytes 5242880 | tf_op jit(solution)/shard_map/all_gather | solution.py:51
  7.3 158.9 %copy-start.2 = (f32[1,32,1024]{2,1,0:T(8,128)S(1)}, f32[1,32,1024]{2,1,0:T(8,128)}, u32[]{:S(2)}) copy-start(f32[1,32,1024]{2,1,0:T(8,128)} %param.12) | copy-start | bytes 393220
  7.3 174.4 %copy-start.4 = (s32[1,32,8]{1,2,0:T(8,128)S(1)}, s32[1,32,8]{1,2,0:T(8,128)}, u32[]{:S(2)}) copy-start(s32[1,32,8]{1,2,0:T(8,128)} %param.15) | copy-start | bytes 3076
  7.3 174.4 %copy-start.5 = (s32[1,32,8]{1,2,0:T(8,128)S(1)}, s32[1,32,8]{1,2,0:T(8,128)}, u32[]{:S(2)}) copy-start(s32[1,32,8]{1,2,0:T(8,128)} %param.14) | copy-start | bytes 3076
  7.3 186.1 %dynamic-slice-start = ((f32[4096]{0:T(1024)}, s32[]{:T(128)}), f32[1024]{0:T(1024)S(1)}, s32[]{:S(2)}) async-start(f32[4096]{0:T(1024)} %param.13, s32[]{:T(128)} %select_n.51), calls=%async_computation.6 | async-start | bytes 8704 | tf_op jit(solution)/shard_map/dynamic_slice | solution.py:33
  166.2 13.9 %collective-permute-start = (f32[32,4096]{1,0:T(8,128)S(1)}, f32[32,4096]{1,0:T(8,128)S(1)}, u32[]{:S(2)}, u32[]{:S(2)}) collective-permute-start(f32[32,4096]{1,0:T(8,128)S(1)} %fusion.23), channel_id=1, source_target_pairs={{0,4},{4,0},{8,12},{12,8},{1,5},{5,1},{9,13},{13,9},{2,6},{6,2},{1... | collective-permute-start | bytes 1572872 | tf_op jit(solution)/shard_map/ppermute | solution.py:28
  180.2 13.0 %collective-permute-start.1 = (f32[32,4096]{1,0:T(8,128)S(1)}, f32[32,4096]{1,0:T(8,128)S(1)}, u32[]{:S(2)}, u32[]{:S(2)}) collective-permute-start(f32[32,4096]{1,0:T(8,128)S(1)} %add.85), channel_id=1, source_target_pairs={{0,8},{4,12},{8,0},{12,4},{1,9},{5,13},{9,1},{13,5},{2,10},{6,14},... | collective-permute-start | bytes 1572872 | tf_op jit(solution)/shard_map/ppermute | solution.py:28
  225.4 144.4 %reduce-scatter.2.cloned.1.call-start = ((), (), s32[]{:S(2)}) async-start(), calls=%async_computation.5 | async-start | bytes 5242880 | tf_op jit(solution)/shard_map/reduce_scatter | solution.py:59
  317.0 59.9 %copy-start.3 = (f32[1,32,8]{1,2,0:T(8,128)S(1)}, f32[1,32,8]{1,2,0:T(8,128)}, u32[]{:S(2)}) copy-start(f32[1,32,8]{1,2,0:T(8,128)} %param.16) | copy-start | bytes 3076
  372.1 30.6 %all-to-all-start.1 = ((bf16[32,12,1024]{2,1,0:T(8,128)(2,1)}), bf16[32,12,1024]{2,1,0:T(8,128)(2,1)S(1)}, u32[]{:S(2)}, u32[]{:S(2)}) async-start(bf16[32,12,1024]{2,1,0:T(8,128)(2,1)} %bitcast.14), calls=%async_computation.2 | async-start | bytes 2097152 | tf_op jit(solution)/shard_map/all_to_all | solution.py:62
  402.8 2.3 copy-start.1
Sparse Core Ops, SparseCore 0:
  8.9 152.3 all-gather.2
  225.5 50.9 all-gather.4
  317.1 52.5 reduce-scatter.1
